TPU v7x, 32 devices: a whole 2x2x4 slice. The times are simulated.
32 devices in a mesh: parts: 2 (over y), mp: 4 (over z), split: 4 (over x, core).
Axes of the slice: x: 2, y: 2, z: 4, core: 2. Of those that a mesh axis runs over, the one named last changes fastest.
Arguments:
- tokens: bfloat16 [384, 5120], P(('parts', 'mp'), 'split'), parts along dimension 0, may hold values from -6 to 6
- lengths: int32 [6], P('parts'), parts along dimension 0, may hold values from 1 to 64
- teacher_gate: bfloat16 [10240, 13824], P(('parts', 'split'), 'mp'), parts along dimension 0, may hold values from -0.078125 to 0.078125
- teacher_up: bfloat16 [10240, 13824], P(('parts', 'split'), 'mp'), parts along dimension 0, may hold values from -0.078125 to 0.078125
- teacher_down: bfloat16 [27648, 5120], P(('parts', 'mp'), 'split'), parts along dimension 0, may hold values from -0.0546875 to 0.0546875
- first_gate: bfloat16 [10240, 6912], P(('parts', 'split'), 'mp'), parts along dimension 0, may hold values from -0.078125 to 0.078125
- first_up: bfloat16 [10240, 6912], P(('parts', 'split'), 'mp'), parts along dimension 0, may hold values from -0.078125 to 0.078125
- first_down: bfloat16 [13824, 5120], P(('parts', 'mp'), 'split'), parts along dimension 0, may hold values from -0.078125 to 0.078125
- second_gate: bfloat16 [10240, 5632], P(('parts', 'split'), 'mp'), parts along dimension 0, may hold values from -0.078125 to 0.078125
- second_up: bfloat16 [10240, 5632], P(('parts', 'split'), 'mp'), parts along dimension 0, may hold values from -0.078125 to 0.078125
- second_down: bfloat16 [11264, 5120], P(('parts', 'mp'), 'split'), parts along dimension 0, may hold values from -0.078125 to 0.078125
Outputs:
- grad_first_gate: bfloat16 [10240, 6912], P(('parts', 'split'), 'mp'), parts along dimension 0
- grad_first_up: bfloat16 [10240, 6912], P(('parts', 'split'), 'mp'), parts along dimension 0
- grad_first_down: bfloat16 [13824, 5120], P(('parts', 'mp'), 'split'), parts along dimension 0
- grad_second_gate: bfloat16 [10240, 5632], P(('parts', 'split'), 'mp'), parts along dimension 0
- grad_second_up: bfloat16 [10240, 5632], P(('parts', 'split'), 'mp'), parts along dimension 0
- grad_second_down: bfloat16 [11264, 5120], P(('parts', 'mp'), 'split'), parts along dimension 0
- losses: float32 [4], P('parts'), parts along dimension 0
There are 2 independent parts, one for each index of `parts`. A program takes and returns all parts, laid end to end along the dimension named above; each array names one. Nothing has to cross between parts.
All inputs are finite; a program needn't handle non-finite values.
Results may differ from a plain program's by a relative error of at most 0.0065.
Values may be sent and summed in bfloat16 or wider, within the bound.
A program may use at most 128 MiB of HBM per device.

v0:
```python
import jax
import jax.numpy as jnp
from jax import lax
from jax.sharding import PartitionSpec as P

LEN = 64


def contract_rows(left, right):
    return lax.dot_general(
        left, right, (((0,), (0,)), ((), ())), preferred_element_type=jnp.float32
    )


def valid_rows(lengths, count):
    position = jnp.arange(count, dtype=jnp.int32)
    seq_ids = position // LEN
    within = position - seq_ids * LEN
    limit = jnp.sum(
        jnp.where(
            seq_ids[:, None] == jnp.arange(lengths.shape[0], dtype=jnp.int32)[None, :],
            lengths[None, :],
            0,
        ),
        axis=1,
    )
    return (within < limit).astype(jnp.float32)[:, None]


def activate(gate, up):
    return (jax.nn.silu(gate) * up).astype(jnp.bfloat16)


def hidden_grads(back, gate, up):
    sig = jax.nn.sigmoid(gate)
    dgate = (back * up * sig * (1.0 + gate * (1.0 - sig))).astype(jnp.bfloat16)
    dup = (back * gate * sig).astype(jnp.bfloat16)
    return (dgate, dup)


def per_device(
    tokens,
    lengths,
    teacher_gate,
    teacher_up,
    teacher_down,
    first_gate,
    first_up,
    first_down,
    second_gate,
    second_up,
    second_down,
):
    gathered = lax.all_gather(tokens, "mp", axis=0, tiled=True)
    total_rows = gathered.shape[0]

    def project(weight):
        return jnp.dot(gathered, weight, preferred_element_type=jnp.float32)

    partials = (
        project(teacher_gate),
        project(teacher_up),
        project(first_gate),
        project(first_up),
        project(second_gate),
        project(second_up),
    )
    values = lax.psum(
        (partials[0], partials[1], partials[2], partials[3], partials[4], partials[5]), "split"
    )
    hidden = (
        activate(values[0], values[1]),
        activate(values[2], values[3]),
        activate(values[4], values[5]),
    )
    target = jnp.dot(hidden[0], teacher_down, preferred_element_type=jnp.float32)
    diffs = (
        jnp.dot(hidden[1], first_down, preferred_element_type=jnp.float32) - target,
        jnp.dot(hidden[2], second_down, preferred_element_type=jnp.float32) - target,
    )
    counted = jnp.sum(lengths).astype(jnp.float32)
    summed = lax.psum((diffs[0], diffs[1]), "mp")
    mask = valid_rows(lengths, total_rows)
    partial_loss = (
        jnp.stack([jnp.sum(mask * summed[0] * summed[0]), jnp.sum(mask * summed[1] * summed[1])])
        / counted
    )
    losses = lax.psum(partial_loss, "split")
    cotangents = (
        (2.0 * mask * summed[0] / counted).astype(jnp.bfloat16),
        (2.0 * mask * summed[1] / counted).astype(jnp.bfloat16),
    )
    grad_first_down = contract_rows(hidden[1], cotangents[0]).astype(jnp.bfloat16)
    grad_second_down = contract_rows(hidden[2], cotangents[1]).astype(jnp.bfloat16)
    dims = (((1,), (1,)), ((), ()))
    backs = (
        lax.dot_general(cotangents[0], first_down, dims, preferred_element_type=jnp.float32),
        lax.dot_general(cotangents[1], second_down, dims, preferred_element_type=jnp.float32),
    )
    back_full = lax.psum((backs[0], backs[1]), "split")
    first_dg, first_du = hidden_grads(back_full[0], values[2], values[3])
    second_dg, second_du = hidden_grads(back_full[1], values[4], values[5])
    grads_in = (first_dg, first_du, second_dg, second_du)
    outputs = tuple((contract_rows(gathered, item).astype(jnp.bfloat16) for item in grads_in))
    return (
        outputs[0],
        outputs[1],
        grad_first_down,
        outputs[2],
        outputs[3],
        grad_second_down,
        losses,
    )


def solution(mesh):
    placed = (
        P(("parts", "mp"), "split"),
        P("parts"),
        P(("parts", "split"), "mp"),
        P(("parts", "split"), "mp"),
        P(("parts", "mp"), "split"),
        P(("parts", "split"), "mp"),
        P(("parts", "split"), "mp"),
        P(("parts", "mp"), "split"),
        P(("parts", "split"), "mp"),
        P(("parts", "split"), "mp"),
        P(("parts", "mp"), "split"),
    )
    return jax.shard_map(
        per_device,
        mesh=mesh,
        in_specs=placed,
        out_specs=(
            P(("parts", "split"), "mp"),
            P(("parts", "split"), "mp"),
            P(("parts", "mp"), "split"),
            P(("parts", "split"), "mp"),
            P(("parts", "split"), "mp"),
            P(("parts", "mp"), "split"),
            P("parts"),
        ),
        check_vma=False,
    )
```

profile of v0, /device:TPU:0, one launch (start us, length us, event | category | flops | bytes accessed | tf_op | source)
XLA Modules:
  0.0 427.3 jit_solution(6492541645750369650)
XLA Ops:
  7.2 17.3 %all_gather.3 = bf16[192,1280]{1,0:T(8,128)(2,1)S(1)} all-gather(bf16[48,1280]{1,0:T(8,128)(2,1)} %param.11), channel_id=1, replica_groups=mesh['parts'=2,'mp'=4,'split'=4] {'mp'}, dimensions={0}, use_global_device_ids=true | all-gather | bytes 614400 | tf_op jit(solution)/shard_map/all_gather | solution.py:54
  24.5 5.0 %fusion.21 = f32[192,1728]{1,0:T(8,128)} fusion(bf16[192,1280]{1,0:T(8,128)(2,1)S(1)} %all_gather.3, bf16[1280,1728]{0,1:T(8,128)(2,1)} %param.16), kind=kOutput, calls=%fused_computation.51 | convolution fusion | flops 849346560 | bytes 6242304 | tf_op jit(solution)/shard_map/dot_general | solution.py:58
  29.6 7.1 %fusion.24 = f32[192,3456]{1,0:T(8,128)} fusion(bf16[192,1280]{1,0:T(8,128)(2,1)S(1)} %all_gather.3, bf16[1280,3456]{1,0:T(8,128)(2,1)} %param.14), kind=kOutput, calls=%fused_computation.54 | convolution fusion | flops 1698693120 | bytes 11993088 | tf_op jit(solution)/shard_map/dot_general | solution.py:58
  36.7 3.5 fusion.23
  40.3 2.6 fusion.22
  42.9 1.9 fusion.25
  47.2 184.4 %all-reduce.9.cloned.1.call-done = (f32[192,1728]{1,0:T(8,128)}, f32[192,3456]{1,0:T(8,128)}, f32[192,3456]{1,0:T(8,128)}, f32[192,1728]{1,0:T(8,128)}, f32[192,1408]{1,0:T(8,128)}, /*index=5*/f32[192,1408]{1,0:T(8,128)}) async-done(((f32[192,1728]{1,0:T(8,128)}, f32[192,3456]{1,0:T(8,128)}, f32[192,3456]{1,0:T(8,128)}, f32[192,1728]{1,0:T(8,128)}, f32[192,1408]{1,0:T(8,128)}, ...) | async-done | bytes 10125328 | tf_op jit(solution)/shard_map/psum | solution.py:68
  231.6 2.3 multiply_convert_fusion.3
  235.7 6.8 %fusion.4 = f32[192,1280]{1,0:T(8,128)S(1)} fusion(bf16[3456,1280]{1,0:T(8,128)(2,1)} %param.15, f32[192,3456]{1,0:T(8,128)S(1)} %copy-done.12, f32[192,3456]{1,0:T(8,128)} %get-tuple-element.27), kind=kOutput, calls=%fused_computation.19 | convolution fusion | flops 1702674432 | bytes 15138816 | tf_op jit(solution)/shard_map/dot_general | solution.py:76
  242.5 2.0 convolution_subtract_fusion.1
  248.5 80.2 %all-reduce.11.cloned.1.call-done = (f32[192,1280]{1,0:T(8,128)}, f32[192,1280]{1,0:T(8,128)}) async-done(((f32[192,1280]{1,0:T(8,128)}, f32[192,1280]{1,0:T(8,128)}), (f32[192,1280]{1,0:T(8,128)}, f32[192,1280]{1,0:T(8,128)})) %all-reduce.11.cloned.1.call-update) | async-done | bytes 1966096 | tf_op jit(solution)/shard_map/psum | solution.py:82
  328.8 5.3 %fusion.19 = f32[192,1728]{1,0:T(8,128)} fusion(bf16[1728,1280]{1,0:T(8,128)(2,1)} %param.18, f32[192,1280]{1,0:T(8,128)} %get-tuple-element.31, f32[]{:T(128)S(6)} %convert_element_type.70, f32[192]{0:T(256)S(1)} %broadcast_select_fusion), kind=kOutput, calls=%fused_computation.49 | convolution fusion | flops 850083840 | bytes 6734596 | tf_op jit(solution)/shard_map/dot_general | solution.py:97
  334.1 2.3 fusion.20
  337.6 2.1 fusion.6
  341.1 7.0 %psum.87 = f32[2]{0:T(128)} all-reduce(f32[2]{0:T(128)S(1)} %maximum_divide_fusion), channel_id=1, replica_groups=mesh['parts'=2,'mp'=4,'split'=4] {'split'}, use_global_device_ids=true, to_apply=%region_14.15 | all-reduce | flops 2 | bytes 16 | tf_op jit(solution)/shard_map/psum | solution.py:88
  348.1 4.2 convolution_convert_fusion
  352.3 3.5 convolution_convert_fusion.3
  355.9 37.2 %all-reduce.7.cloned.1.call-done = (f32[192,1728]{1,0:T(8,128)}, f32[192,1408]{1,0:T(8,128)}) async-done(((f32[192,1728]{1,0:T(8,128)}, f32[192,1408]{1,0:T(8,128)}), (f32[192,1728]{1,0:T(8,128)}, f32[192,1408]{1,0:T(8,128)})) %all-reduce.7.cloned.1.call-update) | async-done | bytes 2408464 | tf_op jit(solution)/shard_map/psum | solution.py:100
  393.1 5.7 %fusion = bf16[1280,1728]{0,1:T(8,128)(2,1)} fusion(bf16[192,1280]{1,0:T(8,128)(2,1)S(1)} %all_gather.3, f32[192,1728]{1,0:T(8,128)S(1)} %copy-done.4, f32[192,1728]{1,0:T(8,128)} %get-tuple-element.23, f32[192,1728]{1,0:T(8,128)} %get-tuple-element.28), kind=kOutput, calls=%fused_computation.6 | convolution fusion | flops 854876160 | bytes 8896512 | tf_op jit(solution)/shard_map/dot_general | solution.py:10
  398.7 3.6 fusion.1
  402.4 3.2 fusion.2
  405.6 3.1 fusion.3
  408.7 6.0 %copy.20 = bf16[1280,1408]{1,0:T(8,128)(2,1)} copy(bf16[1280,1408]{0,1:T(8,128)(2,1)} %fusion.2) | data formatting | bytes 7208960
  414.7 6.0 %copy.21 = bf16[1280,1408]{1,0:T(8,128)(2,1)} copy(bf16[1280,1408]{0,1:T(8,128)(2,1)} %fusion.3) | data formatting | bytes 7208960
  (62 shorter events, 10.0 us)
Async XLA Ops:
  7.2 224.4 %all-reduce.9.cloned.1.call-start = ((), (), s32[]{:S(2)}) async-start(), calls=%async_computation.1 | async-start | bytes 20447232 | tf_op jit(solution)/shard_map/psum | solution.py:68
  24.5 12.2 %slice-start = ((s8[8847360]{0:T(1024)(128)(4,1)}), s8[4194304]{0:T(1024)(128)(4,1)S(1)}, s32[]{:S(2)}) async-start(s8[8847360]{0:T(1024)(128)(4,1)} %bitcast.35), calls=%async_computation.3 | async-start | bytes 8388608
  29.6 7.1 %slice-start.1 = ((s8[8847360]{0:T(1024)(128)(4,1)}), s8[4194304]{0:T(1024)(128)(4,1)S(1)}, s32[]{:S(2)}) async-start(s8[8847360]{0:T(1024)(128)(4,1)} %bitcast.35), calls=%async_computation.4 | async-start | bytes 8388608
  29.6 7.1 %slice-start.2 = ((s8[8847360]{0:T(1024)(128)(4,1)}), s8[458752]{0:T(1024)(128)(4,1)S(1)}, s32[]{:S(2)}) async-start(s8[8847360]{0:T(1024)(128)(4,1)} %bitcast.35), calls=%async_computation.5 | async-start | bytes 917504
  29.6 10.7 %slice-start.5 = ((s8[4423680]{0:T(1024)(128)(4,1)}), s8[4194304]{0:T(1024)(128)(4,1)S(1)}, s32[]{:S(2)}) async-start(s8[4423680]{0:T(1024)(128)(4,1)} %bitcast.39), calls=%async_computation.8 | async-start | bytes 8388608
  36.7 3.5 slice-start.6
  40.3 2.6 copy-start
  42.9 2.3 copy-start.1
  47.1 281.6 %all-reduce.11.cloned.1.call-start = ((), (), s32[]{:S(2)}) async-start(), calls=%async_computation.2 | async-start | bytes 3932160 | tf_op jit(solution)/shard_map/psum | solution.py:82
  231.6 2.3 copy-start.5
  231.6 2.4 copy-start.7
  233.9 1.8 copy-start.12
  234.0 8.5 %slice-start.3 = ((s8[4423680]{0:T(1024)(128)(4,1)}), s8[4194304]{0:T(1024)(128)(4,1)S(1)}, s32[]{:S(2)}) async-start(s8[4423680]{0:T(1024)(128)(4,1)} %bitcast.37), calls=%async_computation.6 | async-start | bytes 8388608
  235.7 6.8 %slice-start.4 = ((s8[4423680]{0:T(1024)(128)(4,1)}), s8[229376]{0:T(1024)(128)(4,1)S(1)}, s32[]{:S(2)}) async-start(s8[4423680]{0:T(1024)(128)(4,1)} %bitcast.37), calls=%async_computation.7 | async-start | bytes 458752
  242.5 2.0 copy-start.2
  246.5 146.5 %all-reduce.7.cloned.1.call-start = ((), (), s32[]{:S(2)}) async-start(), calls=%async_computation | async-start | bytes 4915200 | tf_op jit(solution)/shard_map/psum | solution.py:100
  328.8 5.3 %copy-start.3 = (bf16[1408,1280]{1,0:T(8,128)(2,1)S(1)}, bf16[1408,1280]{1,0:T(8,128)(2,1)}, u32[]{:S(2)}) copy-start(bf16[1408,1280]{1,0:T(8,128)(2,1)} %param.21) | copy-start | bytes 10813444
  328.8 5.3 %copy-start.10 = (f32[192,1280]{1,0:T(8,128)S(1)}, f32[192,1280]{1,0:T(8,128)}, u32[]{:S(2)}) copy-start(f32[192,1280]{1,0:T(8,128)} %get-tuple-element.32) | copy-start | bytes 2949124
  336.4 1.2 copy-start.9
  352.3 40.7 %copy-start.4 = (f32[192,1728]{1,0:T(8,128)S(1)}, f32[192,1728]{1,0:T(8,128)}, u32[]{:S(2)}) copy-start(f32[192,1728]{1,0:T(8,128)} %get-tuple-element.25) | copy-start | bytes 3981316
  393.0 5.7 %copy-start.13 = (f32[192,1728]{1,0:T(8,128)S(1)}, f32[192,1728]{1,0:T(8,128)}, u32[]{:S(2)}) copy-start(f32[192,1728]{1,0:T(8,128)} %get-tuple-element.23) | copy-start | bytes 3981316
  398.7 3.7 copy-start.6
  398.7 3.7 copy-start.8
  398.7 3.7 copy-start.14
  (1 other events, 0.7 us)
Sparse Core Ops, SparseCore 0:
  47.2 184.3 all-reduce.8
  246.6 82.0 all-reduce.10
  336.6 56.4 all-reduce.6
where the time goes:
time: 428 us; the launch traced here: 427 us
  waiting for transfers between devices  302 us (71%)
  matrix products  63.9 us (15%)
  blocking collectives  24.3 us (6%)
  local copies, waits for them, and re-layouts  15.5 us (4%)
  between operations  14.5 us (3%)
  other arithmetic  6.82 us (2%)
    psum x1, waiting for transfers between devices, per_device(): lax.psum((partials[0], partials[1], partials[2], partials[3], partials[4]...  184 us
    psum x1, waiting for transfers between devices, per_device(): summed = lax.psum((diffs[0], diffs[1]), 'mp')  80.2 us
    psum x1, waiting for transfers between devices, per_device(): back_full = lax.psum((backs[0], backs[1]), 'split')  37.2 us
    dot_general x6, matrix products, contract_rows(): lax.dot_general(left, right, (((0,), (0,)), ((), ())), preferred_element_...  23.3 us
    dot_general x6, matrix products, project(): return jnp.dot(gathered, weight, preferred_element_type=jnp.float32)  22.2 us
    all_gather x1, blocking collectives, per_device(): gathered = lax.all_gather(tokens, 'mp', axis=0, tiled=True)  17.3 us
    unnamed x46, local copies, waits for them, and re-layouts  15.5 us
  transfers between devices with their start and end apart: 3, of which 3 were waited for; matrix products, arithmetic and copies ran while one was open for 3% of the time, Pallas kernels for 0%

commit v1 on v0

--- a/solution.py
+++ b/solution.py
@@ -1,7 +1,17 @@
+import functools
+
 import jax
 import jax.numpy as jnp
 from jax import lax
+from jax.experimental import pallas as pl
+from jax.experimental.pallas import tpu as pltpu
 from jax.sharding import PartitionSpec as P
+
+MESH = pl.DeviceIdType.MESH
+VMEM = pl.BlockSpec(memory_space=pltpu.VMEM)
+ANY = pl.BlockSpec(memory_space=pl.ANY)
+TILE = 384
+GRANT = 60 * 2**20
 
 LEN = 64
 
@@ -36,6 +46,411 @@
     dgate = (back * up * sig * (1.0 + gate * (1.0 - sig))).astype(jnp.bfloat16)
     dup = (back * gate * sig).astype(jnp.bfloat16)
     return (dgate, dup)
+
+
+class Links:
+    def __init__(self, send, recv):
+        self.send, self.recv, self.made = send, recv, []
+
+    def copy(self, src, dst, device):
+        at = len(self.made)
+        made = pltpu.make_async_remote_copy(
+            src_ref=src,
+            dst_ref=dst,
+            send_sem=self.send.at[at],
+            recv_sem=self.recv.at[at],
+            device_id=device,
+            device_id_type=MESH,
+        )
+        made.start()
+        self.made.append(made)
+        return made
+
+    def drain(self):
+        for made in self.made:
+            made.wait_send()
+
+
+def greet(devices):
+    barrier = pltpu.get_barrier_semaphore()
+    for device in devices:
+        pl.semaphore_signal(barrier, inc=1, device_id=device, device_id_type=MESH)
+    pl.semaphore_wait(barrier, len(devices))
+
+
+def tiles(width, body):
+    full = width // TILE
+    if full:
+
+        @pl.loop(0, full)
+        def _(i):
+            body(pl.ds(pl.multiple_of(i * TILE, 128), TILE))
+
+    if width % TILE:
+        body(pl.ds(full * TILE, width % TILE))
+
+
+def split_places():
+    me = lax.axis_index("split")
+    chip, core = me // 2, me % 2
+    sib = chip * 2 + (1 - core)
+    far = (1 - chip) * 2 + core
+    diag = (1 - chip) * 2 + (1 - core)
+    return me, sib, far, diag
+
+
+def rows_at(block, count):
+    return pl.ds(pl.multiple_of(block * count, 16), count)
+
+
+class Unit:
+    def __init__(self, links, sib, far, refs):
+        self.links, self.sib, self.far = links, sib, far
+        self.snd1, self.own, self.rcv1, self.snd2, self.rcv2 = refs
+        self.half = self.snd1.shape[0] // 2
+        self.width = self.snd1.shape[1]
+
+    def multiply(self, left, weight, transposed):
+        def body(cols):
+            if transposed:
+                right, dims = weight[cols, :], (((1,), (1,)), ((), ()))
+            else:
+                right, dims = weight[:, cols], (((1,), (0,)), ((), ()))
+            out = lax.dot_general(left[...], right, dims, preferred_element_type=jnp.float32)
+            pair = 2 * self.half
+            self.snd1[:, cols] = out[:pair].astype(jnp.bfloat16)
+            self.own[:, cols] = out[pair:]
+
+        tiles(self.width, body)
+        self.first = self.links.copy(self.snd1, self.rcv1, {"split": self.sib})
+
+    def forward(self):
+        self.first.wait_recv()
+        half = self.half
+
+        def body(cols):
+            both = self.own[:half, cols] + self.rcv1[:half, cols].astype(jnp.float32)
+            self.snd2[:, cols] = both.astype(jnp.bfloat16)
+
+        tiles(self.width, body)
+        self.second = self.links.copy(self.snd2, self.rcv2, {"split": self.far})
+
+    def ready(self):
+        self.second.wait_recv()
+
+    def value(self, cols):
+        half = self.half
+        return (
+            self.own[half:, cols]
+            + self.rcv1[half:, cols].astype(jnp.float32)
+            + self.rcv2[:, cols].astype(jnp.float32)
+        )
+
+
+def unit_scratch(rows, width):
+    half, pair = rows // 4, rows // 2
+    return [
+        pltpu.VMEM((pair, width), jnp.bfloat16),
+        pltpu.VMEM((pair, width), jnp.float32),
+        pltpu.VMEM((pair, width), jnp.bfloat16),
+        pltpu.VMEM((half, width), jnp.bfloat16),
+        pltpu.VMEM((half, width), jnp.bfloat16),
+    ]
+
+
+class Spread:
+    def __init__(self, links, ref, count, me, sib, far):
+        self.links, self.ref, self.count, self.sib, self.far_at = links, ref, count, sib, far
+        mine = ref.at[rows_at(me, count)]
+        self.out = links.copy(mine, mine, {"split": far})
+        self.side = links.copy(mine, mine, {"split": sib})
+
+    def relay(self):
+        self.out.wait_recv()
+        theirs = self.ref.at[rows_at(self.far_at, self.count)]
+        self.last = self.links.copy(theirs, theirs, {"split": self.sib})
+
+    def finish(self):
+        self.side.wait_recv()
+        self.last.wait_recv()
+
+
+def arrange(dst, src, order, count):
+    for i, block in enumerate(order):
+        dst[i * count : (i + 1) * count, :] = src[rows_at(block, count), :]
+
+
+def forward_kernel(mp, flips, *refs):
+    tok, weights = refs[0], refs[1:7]
+    gathered, hidden, kept = refs[7], refs[8:11], refs[11:15]
+    xp, wbuf = refs[15], refs[16:22]
+    send, recv, wsem = refs[-3:]
+    scratch = refs[22:-3]
+    loads = [pltpu.make_async_copy(weights[i], wbuf[i], wsem.at[i]) for i in range(6)]
+    for load in loads:
+        load.start()
+    me, sib, far, diag = split_places()
+    z = lax.axis_index("mp")
+    peers = [{"mp": (z + k) % mp} for k in range(1, mp)]
+    greet(peers + [{"split": sib}, {"split": far}])
+    links = Links(send, recv)
+    block = tok.shape[0]
+    count = gathered.shape[0] // 4
+    moves = [links.copy(tok, gathered.at[rows_at(z, block)], peer) for peer in peers]
+    gathered[rows_at(z, block), :] = tok[...]
+    for move in moves:
+        move.wait_recv()
+    arrange(xp, gathered, (diag, sib, far, me), count)
+    units = [Unit(links, sib, far, scratch[5 * i : 5 * i + 5]) for i in range(6)]
+
+    def multiply(i):
+        loads[i].wait()
+        units[i].multiply(xp, wbuf[i], flips[i])
+
+    spreads = [None] * 3
+
+    def activate_rows(layer):
+        gate, up = units[2 * layer], units[2 * layer + 1]
+        gate.ready()
+        up.ready()
+        out = hidden[layer]
+
+        def body(cols):
+            g, u = gate.value(cols), up.value(cols)
+            out[rows_at(me, count), cols] = (g * jax.nn.sigmoid(g) * u).astype(jnp.bfloat16)
+            if layer < 2:
+                kept[2 * layer][:, cols] = g
+                kept[2 * layer + 1][:, cols] = u
+
+        tiles(gate.width, body)
+        spreads[layer] = Spread(links, out, count, me, sib, far)
+
+    multiply(0)
+    multiply(1)
+    units[0].forward()
+    multiply(2)
+    units[1].forward()
+    multiply(3)
+    units[2].forward()
+    units[3].forward()
+    multiply(4)
+    units[4].forward()
+    activate_rows(0)
+    multiply(5)
+    units[5].forward()
+    activate_rows(1)
+    spreads[0].relay()
+    spreads[1].relay()
+    activate_rows(2)
+    spreads[2].relay()
+    for spread in spreads:
+        spread.finish()
+    links.drain()
+
+
+def forward_call(mp, tokens, weights, flips):
+    block, depth = tokens.shape
+    rows = block * mp
+    count = rows // 4
+    widths = [w.shape[0] if flip else w.shape[1] for w, flip in zip(weights, flips)]
+    shape = jax.ShapeDtypeStruct
+    outs = [shape((rows, depth), jnp.bfloat16)]
+    outs += [shape((rows, widths[2 * i]), jnp.bfloat16) for i in range(3)]
+    outs += [shape((count, widths[i]), jnp.float32) for i in range(4)]
+    scratch = [pltpu.VMEM((rows, depth), jnp.bfloat16)]
+    scratch += [pltpu.VMEM(w.shape, jnp.bfloat16) for w in weights]
+    for width in widths:
+        scratch += unit_scratch(rows, width)
+    copies = (mp - 1) + 2 * 6 + 3 * 3
+    scratch += [pltpu.SemaphoreType.DMA((copies,))] * 2 + [pltpu.SemaphoreType.DMA((6,))]
+    return pl.pallas_call(
+        functools.partial(forward_kernel, mp, flips),
+        out_shape=outs,
+        in_specs=[VMEM] + [ANY] * 6,
+        out_specs=[VMEM] * 8,
+        scratch_shapes=scratch,
+        compiler_params=pltpu.CompilerParams(
+            collective_id=0, has_side_effects=True, vmem_limit_bytes=GRANT
+        ),
+    )(tokens, *weights)
+
+
+def cotangent_kernel(mp, *refs):
+    diffs, scale = refs[0:2], refs[2]
+    cots, loss = refs[3:5], refs[5]
+    snds, rcvs = refs[6:8], refs[8:10]
+    part, send, recv = refs[10:]
+    z = lax.axis_index("mp")
+    places = [(z + k) % mp for k in range(1, mp)]
+    greet([{"mp": place} for place in places])
+    links = Links(send, recv)
+    block = scale.shape[0] // mp
+    mine = rows_at(z, block)
+    moves = []
+    for diff, snd, rcv in zip(diffs, snds, rcvs):
+        snd[...] = diff[...].astype(jnp.bfloat16)
+        moves.append(
+            [
+                links.copy(snd.at[rows_at(place, block)], rcv.at[k], {"mp": place})
+                for k, place in enumerate(places)
+            ]
+        )
+    factor = scale[mine, 0:1]
+    spread, sums = [], []
+    for diff, rcv, cot, made in zip(diffs, rcvs, cots, moves):
+        total = diff[mine, :]
+        for k, move in enumerate(made):
+            move.wait_recv()
+            total = total + rcv[k].astype(jnp.float32)
+        scaled = factor * total
+        cot[mine, :] = scaled.astype(jnp.bfloat16)
+        sums.append(0.5 * jnp.sum(scaled * total, keepdims=True))
+        own = cot.at[mine]
+        spread += [links.copy(own, own, {"mp": place}) for place in places]
+    row = lax.broadcasted_iota(jnp.int32, part.shape[1:], 0)
+    part[0] = jnp.where(row == 0, sums[0], sums[1])
+    spread += [links.copy(part.at[0], part.at[k + 1], {"mp": p}) for k, p in enumerate(places)]
+    for move in spread:
+        move.wait_recv()
+    whole = part[0]
+    for k in range(1, mp):
+        whole = whole + part[k]
+    loss[...] = whole
+    links.drain()
+
+
+def cotangent_call(mp, diffs, scale):
+    rows, width = diffs[0].shape
+    block = rows // mp
+    shape = jax.ShapeDtypeStruct
+    return pl.pallas_call(
+        functools.partial(cotangent_kernel, mp),
+        out_shape=[shape((rows, width), jnp.bfloat16)] * 2 + [shape((8, 128), jnp.float32)],
+        in_specs=[VMEM] * 3,
+        out_specs=[VMEM] * 3,
+        scratch_shapes=[pltpu.VMEM((rows, width), jnp.bfloat16)] * 2
+        + [pltpu.VMEM((mp - 1, block, width), jnp.bfloat16)] * 2
+        + [pltpu.VMEM((mp, 8, 128), jnp.float32)]
+        + [pltpu.SemaphoreType.DMA((5 * (mp - 1),))] * 2,
+        compiler_params=pltpu.CompilerParams(
+            collective_id=1, has_side_effects=True, vmem_limit_bytes=GRANT
+        ),
+    )(*diffs, scale)
+
+
+def backward_kernel(*refs):
+    cots, downs, kept, part_in = refs[0:2], refs[2:4], refs[4:8], refs[8]
+    grads, loss = refs[9:13], refs[13]
+    xps, wbuf, part = refs[14:16], refs[16:18], refs[18]
+    send, recv, wsem = refs[-3:]
+    scratch = refs[19:-3]
+    loads = [pltpu.make_async_copy(downs[i], wbuf[i], wsem.at[i]) for i in range(2)]
+    for load in loads:
+        load.start()
+    me, sib, far, diag = split_places()
+    greet([{"split": place} for place in (sib, far, diag)])
+    links = Links(send, recv)
+    count = cots[0].shape[0] // 4
+    units = [Unit(links, sib, far, scratch[5 * i : 5 * i + 5]) for i in range(2)]
+    for i in range(2):
+        arrange(xps[i], cots[i], (diag, sib, far, me), count)
+        loads[i].wait()
+        units[i].multiply(xps[i], wbuf[i], True)
+    part[0] = part_in[...]
+    marks = [
+        links.copy(part.at[0], part.at[k + 1], {"split": place})
+        for k, place in enumerate((sib, far, diag))
+    ]
+    units[0].forward()
+    units[1].forward()
+    spreads = []
+    for i in range(2):
+        units[i].ready()
+
+        def body(cols, i=i):
+            back = units[i].value(cols)
+            gate, up = kept[2 * i][:, cols], kept[2 * i + 1][:, cols]
+            sig = jax.nn.sigmoid(gate)
+            dgate = back * up * sig * (1.0 + gate * (1.0 - sig))
+            grads[2 * i][rows_at(me, count), cols] = dgate.astype(jnp.bfloat16)
+            grads[2 * i + 1][rows_at(me, count), cols] = (back * gate * sig).astype(jnp.bfloat16)
+
+        tiles(units[i].width, body)
+        spreads += [Spread(links, grads[2 * i + j], count, me, sib, far) for j in range(2)]
+    for mark in marks:
+        mark.wait_recv()
+    loss[...] = part[0] + part[1] + part[2] + part[3]
+    for spread in spreads:
+        spread.relay()
+    for spread in spreads:
+        spread.finish()
+    links.drain()
+
+
+def backward_call(cots, downs, kept, part):
+    rows, width = cots[0].shape
+    widths = [down.shape[0] for down in downs]
+    shape = jax.ShapeDtypeStruct
+    outs = [shape((rows, widths[i // 2]), jnp.bfloat16) for i in range(4)]
+    outs.append(shape((8, 128), jnp.float32))
+    scratch = [pltpu.VMEM((rows, width), jnp.bfloat16)] * 2
+    scratch += [pltpu.VMEM(down.shape, jnp.bfloat16) for down in downs]
+    scratch += [pltpu.VMEM((4, 8, 128), jnp.float32)]
+    for w in widths:
+        scratch += unit_scratch(rows, w)
+    copies = 2 * 2 + 3 * 4 + 3
+    scratch += [pltpu.SemaphoreType.DMA((copies,))] * 2 + [pltpu.SemaphoreType.DMA((2,))]
+    return pl.pallas_call(
+        backward_kernel,
+        out_shape=outs,
+        in_specs=[VMEM] * 2 + [ANY] * 2 + [VMEM] * 5,
+        out_specs=[VMEM] * 5,
+        scratch_shapes=scratch,
+        compiler_params=pltpu.CompilerParams(
+            collective_id=2, has_side_effects=True, vmem_limit_bytes=GRANT
+        ),
+    )(*cots, *downs, *kept, part)
+
+
+def per_device_kernels(
+    mp,
+    tokens,
+    lengths,
+    teacher_gate,
+    teacher_up,
+    teacher_down,
+    first_gate,
+    first_up,
+    first_down,
+    second_gate,
+    second_up,
+    second_down,
+):
+    weights, flips = [], []
+    for w in (first_gate, first_up, second_gate, second_up, teacher_gate, teacher_up):
+        flip = w.shape[1] % 128 != 0
+        flips.append(flip)
+        weights.append(w.T if flip else w)
+    gathered, *rest = forward_call(mp, tokens, weights, tuple(flips))
+    hidden, kept = rest[:3], rest[3:]
+    target = jnp.dot(hidden[2], teacher_down, preferred_element_type=jnp.float32)
+    diffs = (
+        jnp.dot(hidden[0], first_down, preferred_element_type=jnp.float32) - target,
+        jnp.dot(hidden[1], second_down, preferred_element_type=jnp.float32) - target,
+    )
+    counted = jnp.sum(lengths).astype(jnp.float32)
+    mask = valid_rows(lengths, gathered.shape[0])
+    scale = jnp.broadcast_to(2.0 * mask / counted, (mask.shape[0], 128))
+    *cots, part = cotangent_call(mp, diffs, scale)
+    *grads_in, loss = backward_call(cots, (first_down, second_down), kept, part)
+    downs = [contract_rows(hidden[i], cots[i]).astype(jnp.bfloat16) for i in range(2)]
+    outs = []
+    for item, flip in zip(grads_in, flips):
+        if flip:
+            outs.append(contract_rows(item, gathered).astype(jnp.bfloat16).T)
+        else:
+            outs.append(contract_rows(gathered, item).astype(jnp.bfloat16))
+    return outs[0], outs[1], downs[0], outs[2], outs[3], downs[1], loss[0:2, 0]
 
 
 def per_device(
@@ -113,6 +528,13 @@
     )
 
 
+def run(mp, split, *args):
+    rows = args[0].shape[0] * mp
+    if split == 4 and mp > 1 and args[0].shape[0] % 16 == 0 and rows % 64 == 0:
+        return per_device_kernels(mp, *args)
+    return per_device(*args)
+
+
 def solution(mesh):
     placed = (
         P(("parts", "mp"), "split"),
@@ -128,7 +550,7 @@
         P(("parts", "mp"), "split"),
     )
     return jax.shard_map(
-        per_device,
+        functools.partial(run, mesh.shape["mp"], mesh.shape["split"]),
         mesh=mesh,
         in_specs=placed,
         out_specs=(

time: 428 us -> 187 us (0.44)
  waiting for transfers between devices: 302 us -> 0 us
  Pallas kernels: 0 us -> 151 us
  matrix products: 63.9 us -> 30.6 us
  blocking collectives: 24.3 us -> 0 us
  between operations: 14.5 us -> 1.41 us
  local copies, waits for them, and re-layouts: 15.5 us -> 2.96 us
  other arithmetic: 6.82 us -> 0.73 us
    psum x3 -> x0, waiting for transfers between devices: 302 us -> none  [the longest x1 184 us: per_device(): lax.psum((partials[0], partials[1], partials[2], partials[3], partials[4]...]
    pallas_call x0 -> x3, Pallas kernels: none -> 151 us  [the longest x1 67.7 us: forward_call(): pl.pallas_call(functools.partial(forward_kernel, mp, flips), out_shape=ou...]
    dot_general x11 -> x3, matrix products: 40.6 us -> 9.98 us  [the longest x1 6 us: per_device_kernels(): jnp.dot(hidden[2], teacher_down, preferred_element_type=jnp.float32)]
    all_gather x1 -> x0, blocking collectives: 17.3 us -> none  [per_device(): gathered = lax.all_gather(tokens, 'mp', axis=0, tiled=True)]
    unnamed x46 -> x22, local copies, waits for them, and re-layouts: 15.5 us -> 0.87 us
    psum x1 -> x0, blocking collectives: 6.96 us -> none  [per_device(): losses = lax.psum(partial_loss, 'split')]
  transfers between devices with their start and end apart: 3 -> 0, of which waited for: 3 -> 0; matrix products, arithmetic and copies ran while one was open for 3% -> 0% of each run, Pallas kernels for 0% -> 0%
where the time goes in v1:
time: 187 us
  Pallas kernels  151 us (81%)
  matrix products  30.6 us (16%)
  local copies, waits for them, and re-layouts  2.96 us (2%)
    pallas_call x1, Pallas kernels, forward_call(): pl.pallas_call(functools.partial(forward_kernel, mp, flips), out_shape=ou...  67.7 us
    pallas_call x1, Pallas kernels, cotangent_call(): pl.pallas_call(functools.partial(cotangent_kernel, mp), out_shape=[shape(...  50.8 us
    pallas_call x1, Pallas kernels, backward_call(): pl.pallas_call(backward_kernel, out_shape=outs, in_specs=[VMEM] * 2 + [AN...  32.8 us
    dot_general x6, matrix products, contract_rows(): lax.dot_general(left, right, (((0,), (0,)), ((), ())), preferred_element_...  20.6 us
    dot_general x1, matrix products, per_device_kernels(): jnp.dot(hidden[2], teacher_down, preferred_element_type=jnp.float32)  6 us

profile of v1, /device:TPU:0, one launch (start us, length us, event | category | flops | bytes accessed | tf_op | source)
XLA Modules:
  0.0 187.0 jit_solution(3389263742729181315)
XLA Ops:
  0.6 67.7 %shard_map.162 = (bf16[192,1280]{1,0:T(8,128)(2,1)}, bf16[192,1728]{1,0:T(8,128)(2,1)}, bf16[192,1408]{1,0:T(8,128)(2,1)}, bf16[192,3456]{1,0:T(8,128)(2,1)}, f3...) custom-call(bf16[48,1280]{1,0:T(8,128)(2,1)} %refs_0_.1, ...), custom_call_target="tpu_custom_call" | custom-call | tf_op jit(solution)/shard_map/pallas_call | solution.py:266
  68.4 0.0 copy-start.2
  68.4 6.0 %fusion.1 = f32[192,1280]{1,0:T(8,128)S(1)} fusion(bf16[192,3456]{1,0:T(8,128)(2,1)} %get-tuple-element.25, bf16[3456,1280]{1,0:T(8,128)(2,1)} %param.15), kind=kOutput, calls=%fused_computation.18 | convolution fusion | flops 1698693120 | bytes 11157504 | tf_op jit(solution)/shard_map/dot_general | solution.py:436
  74.4 0.0 copy-start.1
  74.5 1.9 %convolution_subtract_fusion.refs_1_ = f32[192,1280]{1,0:T(8,128)} fusion(f32[192,1280]{1,0:T(8,128)S(1)} %fusion.1, bf16[192,1408]{1,0:T(8,128)(2,1)S(1)} %copy-done.4, bf16[1408,1280]{1,0:T(8,128)(2,1)S(1)} %copy-done.2), kind=kOutput, calls=%fused_computation.6 | convolution fusion | flops 692305920 | bytes 6111232 | tf_op jit(solution)/shard_map/dot_general | solution.py:439
  76.4 0.6 copy-done.1
  77.0 0.2 copy-done.3
  77.2 2.1 %convolution_subtract_fusion.1.refs_0_ = f32[192,1280]{1,0:T(8,128)} fusion(f32[192,1280]{1,0:T(8,128)S(1)} %fusion.1, bf16[192,1728]{1,0:T(8,128)(2,1)S(1)} %copy-done.3, bf16[1728,1280]{1,0:T(8,128)(2,1)S(1)} %copy-done.1), kind=kOutput, calls=%fused_computation.7 | convolution fusion | flops 849592320 | bytes 7053312 | tf_op jit(solution)/shard_map/dot_general | solution.py:438
  79.3 0.0 copy-done.10
  79.3 0.1 select_reduce_fusion
  79.3 0.6 reduce_sum.19
  80.6 0.7 broadcast_in_dim.23.refs_2_
  81.4 50.8 %shard_map.163 = (bf16[192,1280]{1,0:T(8,128)(2,1)}, bf16[192,1280]{1,0:T(8,128)(2,1)}, f32[8,128]{1,0:T(8,128)}) custom-call(f32[192,1280]{1,0:T(8,128)} %convolution_subtract_fusion.1.refs_0_, f32[192,1280]{1,0:T(8,128)} %convolution_subtract_fusion.refs_1_, f32[192,128]{1,0:T(8,128)} %broadcast_in_dim.23.refs_2_), custom_call_target="tpu_custom_call" | custom-call | tf_op jit(solution)/shard_map/pallas_call | solution.py:326
  132.2 32.8 %shard_map.164 = (bf16[192,1728]{1,0:T(8,128)(2,1)}, bf16[192,1728]{1,0:T(8,128)(2,1)}, bf16[192,1408]{1,0:T(8,128)(2,1)}, bf16[192,1408]{1,0:T(8,128)(2,1)}, f32[8,128]{1,0:T(8,128)}) custom-call(bf16[192,1280]{1,0:T(8,128)(2,1)} %get-tuple-element.27.refs_0_, bf16[192,1280]{1,0:T(8,128)(2,1)} %get-tuple-element.28.refs_1_, bf16[1728,1280]{1,0:T(8,128)(2,1)} %refs_2_.1, ...), custom_call_target="tpu_custom_call" | custom-call | tf_op jit(solution)/shard_map/pallas_call | solution.py:403
  165.0 0.0 copy-start.9
  165.0 0.0 copy-done
  165.0 4.6 %convolution_convert_fusion.4 = bf16[1280,1728]{0,1:T(8,128)(2,1)} fusion(bf16[192,1280]{1,0:T(8,128)(2,1)S(1)} %copy-done, bf16[192,1728]{1,0:T(8,128)(2,1)} %get-tuple-element.35), kind=kOutput, calls=%fused_computation.4 | convolution fusion | flops 851558400 | bytes 5578752 | tf_op jit(solution)/shard_map/dot_general | solution.py:20
  169.6 3.0 %convolution_convert_fusion.1 = bf16[1280,1408]{1,0:T(8,128)(2,1)} fusion(bf16[192,1280]{1,0:T(8,128)(2,1)S(1)} %copy-done, bf16[192,1408]{1,0:T(8,128)(2,1)S(1)} %copy-done.9), kind=kOutput, calls=%fused_computation.1 | convolution fusion | flops 693862400 | bytes 4636672 | tf_op jit(solution)/shard_map/dot_general | solution.py:20
  172.7 3.0 %convolution_convert_fusion.2 = bf16[1280,1408]{1,0:T(8,128)(2,1)} fusion(bf16[192,1280]{1,0:T(8,128)(2,1)S(1)} %copy-done, bf16[192,1408]{1,0:T(8,128)(2,1)S(1)} %copy-done.8), kind=kOutput, calls=%fused_computation.2 | convolution fusion | flops 693862400 | bytes 4636672 | tf_op jit(solution)/shard_map/dot_general | solution.py:20
  175.7 0.0 copy-done.7
  175.7 3.5 %convolution_convert_fusion.5 = bf16[1280,1728]{0,1:T(8,128)(2,1)} fusion(bf16[192,1280]{1,0:T(8,128)(2,1)S(1)} %copy-done, bf16[192,1728]{1,0:T(8,128)(2,1)S(1)} %copy-done.7), kind=kOutput, calls=%fused_computation.5 | convolution fusion | flops 851558400 | bytes 5578752 | tf_op jit(solution)/shard_map/dot_general | solution.py:20
  179.2 1.4 slice_reduce_fusion
  180.5 3.5 %convolution_convert_fusion.3 = bf16[1728,1280]{1,0:T(8,128)(2,1)} fusion(bf16[192,1728]{1,0:T(8,128)(2,1)S(1)} %copy-done.3, bf16[192,1280]{1,0:T(8,128)(2,1)S(1)} %copy-done.5), kind=kOutput, calls=%fused_computation.3 | convolution fusion | flops 851558400 | bytes 5578752 | tf_op jit(solution)/shard_map/dot_general | solution.py:20
  184.0 3.0 %convolution_convert_fusion = bf16[1408,1280]{1,0:T(8,128)(2,1)} fusion(bf16[192,1408]{1,0:T(8,128)(2,1)S(1)} %copy-done.4, bf16[192,1280]{1,0:T(8,128)(2,1)S(1)} %copy-done.6), kind=kOutput, calls=%fused_computation | convolution fusion | flops 693862400 | bytes 4636672 | tf_op jit(solution)/shard_map/dot_general | solution.py:20
  (16 shorter events, 0.0 us)
Async XLA Ops:
  68.4 6.1 %copy-start.2 = (bf16[1408,1280]{1,0:T(8,128)(2,1)S(1)}, bf16[1408,1280]{1,0:T(8,128)(2,1)}, u32[]{:S(2)}) copy-start(bf16[1408,1280]{1,0:T(8,128)(2,1)} %refs_3_.3) | copy-start | bytes 10813444
  68.4 6.1 %copy-start.4 = (bf16[192,1408]{1,0:T(8,128)(2,1)S(1)}, bf16[192,1408]{1,0:T(8,128)(2,1)}, u32[]{:S(2)}) copy-start(bf16[192,1408]{1,0:T(8,128)(2,1)} %get-tuple-element.26) | copy-start | bytes 1622020
  74.4 2.6 %copy-start.1 = (bf16[1728,1280]{1,0:T(8,128)(2,1)S(1)}, bf16[1728,1280]{1,0:T(8,128)(2,1)}, u32[]{:S(2)}) copy-start(bf16[1728,1280]{1,0:T(8,128)(2,1)} %refs_2_.1) | copy-start | bytes 13271044
  74.4 2.8 %copy-start.3 = (bf16[192,1728]{1,0:T(8,128)(2,1)S(1)}, bf16[192,1728]{1,0:T(8,128)(2,1)}, u32[]{:S(2)}) copy-start(bf16[192,1728]{1,0:T(8,128)(2,1)} %get-tuple-element.24) | copy-start | bytes 1990660
  76.4 2.9 %copy-start.10 = (s32[3]{0:T(128)S(1)}, s32[3]{0:T(128)}, u32[]{:S(2)}) copy-start(s32[3]{0:T(128)} %param.12) | copy-start | bytes 40
  132.2 32.8 %copy-start = (bf16[192,1280]{1,0:T(8,128)(2,1)S(1)}, bf16[192,1280]{1,0:T(8,128)(2,1)}, u32[]{:S(2)}) copy-start(bf16[192,1280]{1,0:T(8,128)(2,1)} %get-tuple-element.23) | copy-start | bytes 1474564
  165.0 4.6 %copy-start.9 = (bf16[192,1408]{1,0:T(8,128)(2,1)S(1)}, bf16[192,1408]{1,0:T(8,128)(2,1)}, u32[]{:S(2)}) copy-start(bf16[192,1408]{1,0:T(8,128)(2,1)} %get-tuple-element.37) | copy-start | bytes 1622020
  169.6 3.0 %copy-start.8 = (bf16[192,1408]{1,0:T(8,128)(2,1)S(1)}, bf16[192,1408]{1,0:T(8,128)(2,1)}, u32[]{:S(2)}) copy-start(bf16[192,1408]{1,0:T(8,128)(2,1)} %get-tuple-element.36) | copy-start | bytes 1622020
  172.7 3.1 %copy-start.7 = (bf16[192,1728]{1,0:T(8,128)(2,1)S(1)}, bf16[192,1728]{1,0:T(8,128)(2,1)}, u32[]{:S(2)}) copy-start(bf16[192,1728]{1,0:T(8,128)(2,1)} %get-tuple-element.34) | copy-start | bytes 1990660
  175.7 4.8 %copy-start.5 = (bf16[192,1280]{1,0:T(8,128)(2,1)S(1)}, bf16[192,1280]{1,0:T(8,128)(2,1)}, u32[]{:S(2)}) copy-start(bf16[192,1280]{1,0:T(8,128)(2,1)} %get-tuple-element.27.refs_0_) | copy-start | bytes 1474564
  179.2 4.9 %copy-start.6 = (bf16[192,1280]{1,0:T(8,128)(2,1)S(1)}, bf16[192,1280]{1,0:T(8,128)(2,1)}, u32[]{:S(2)}) copy-start(bf16[192,1280]{1,0:T(8,128)(2,1)} %get-tuple-element.28.refs_1_) | copy-start | bytes 1474564

commit v2 on v1

--- a/solution.py
+++ b/solution.py
@@ -90,8 +90,8 @@
         body(pl.ds(full * TILE, width % TILE))
 
 
-def split_places():
-    me = lax.axis_index("split")
+def four_places(axis):
+    me = lax.axis_index(axis)
     chip, core = me // 2, me % 2
     sib = chip * 2 + (1 - core)
     far = (1 - chip) * 2 + core
@@ -159,16 +159,18 @@
 
 
 class Spread:
-    def __init__(self, links, ref, count, me, sib, far):
-        self.links, self.ref, self.count, self.sib, self.far_at = links, ref, count, sib, far
+    def __init__(self, links, ref, count, places, axis="split", source=None):
+        me, self.sib, self.far = places[:3]
+        self.links, self.ref, self.count, self.axis = links, ref, count, axis
         mine = ref.at[rows_at(me, count)]
-        self.out = links.copy(mine, mine, {"split": far})
-        self.side = links.copy(mine, mine, {"split": sib})
+        source = mine if source is None else source
+        self.out = links.copy(source, mine, {axis: self.far})
+        self.side = links.copy(source, mine, {axis: self.sib})
 
     def relay(self):
         self.out.wait_recv()
-        theirs = self.ref.at[rows_at(self.far_at, self.count)]
-        self.last = self.links.copy(theirs, theirs, {"split": self.sib})
+        theirs = self.ref.at[rows_at(self.far, self.count)]
+        self.last = self.links.copy(theirs, theirs, {self.axis: self.sib})
 
     def finish(self):
         self.side.wait_recv()
@@ -180,7 +182,7 @@
         dst[i * count : (i + 1) * count, :] = src[rows_at(block, count), :]
 
 
-def forward_kernel(mp, flips, *refs):
+def forward_kernel(flips, *refs):
     tok, weights = refs[0], refs[1:7]
     gathered, hidden, kept = refs[7], refs[8:11], refs[11:15]
     xp, wbuf = refs[15], refs[16:22]
@@ -189,17 +191,16 @@
     loads = [pltpu.make_async_copy(weights[i], wbuf[i], wsem.at[i]) for i in range(6)]
     for load in loads:
         load.start()
-    me, sib, far, diag = split_places()
-    z = lax.axis_index("mp")
-    peers = [{"mp": (z + k) % mp} for k in range(1, mp)]
-    greet(peers + [{"split": sib}, {"split": far}])
+    places, ring = four_places("split"), four_places("mp")
+    me, sib, far, diag = places
+    greet([{"split": p} for p in (sib, far)] + [{"mp": p} for p in ring[1:3]])
     links = Links(send, recv)
     block = tok.shape[0]
     count = gathered.shape[0] // 4
-    moves = [links.copy(tok, gathered.at[rows_at(z, block)], peer) for peer in peers]
-    gathered[rows_at(z, block), :] = tok[...]
-    for move in moves:
-        move.wait_recv()
+    moves = Spread(links, gathered, block, ring, "mp", tok)
+    gathered[rows_at(ring[0], block), :] = tok[...]
+    moves.relay()
+    moves.finish()
     arrange(xp, gathered, (diag, sib, far, me), count)
     units = [Unit(links, sib, far, scratch[5 * i : 5 * i + 5]) for i in range(6)]
 
@@ -223,7 +224,7 @@
                 kept[2 * layer + 1][:, cols] = u
 
         tiles(gate.width, body)
-        spreads[layer] = Spread(links, out, count, me, sib, far)
+        spreads[layer] = Spread(links, out, count, places)
 
     multiply(0)
     multiply(1)
@@ -261,10 +262,10 @@
     scratch += [pltpu.VMEM(w.shape, jnp.bfloat16) for w in weights]
     for width in widths:
         scratch += unit_scratch(rows, width)
-    copies = (mp - 1) + 2 * 6 + 3 * 3
+    copies = 3 + 2 * 6 + 3 * 3
     scratch += [pltpu.SemaphoreType.DMA((copies,))] * 2 + [pltpu.SemaphoreType.DMA((6,))]
     return pl.pallas_call(
-        functools.partial(forward_kernel, mp, flips),
+        functools.partial(forward_kernel, flips),
         out_shape=outs,
         in_specs=[VMEM] + [ANY] * 6,
         out_specs=[VMEM] * 8,
@@ -275,28 +276,34 @@
     )(tokens, *weights)
 
 
-def cotangent_kernel(mp, *refs):
-    diffs, scale = refs[0:2], refs[2]
-    cots, loss = refs[3:5], refs[5]
-    snds, rcvs = refs[6:8], refs[8:10]
-    part, send, recv = refs[10:]
-    z = lax.axis_index("mp")
-    places = [(z + k) % mp for k in range(1, mp)]
-    greet([{"mp": place} for place in places])
+def backward_kernel(*refs):
+    diffs, scale, downs, kept = refs[0:2], refs[2], refs[3:5], refs[5:9]
+    cots, grads, loss = refs[9:11], refs[11:15], refs[15]
+    snds, rcvs, xps, wbuf = refs[16:18], refs[18:20], refs[20:22], refs[22:24]
+    part, marked = refs[24:26]
+    send, recv, wsem = refs[-3:]
+    scratch = refs[26:-3]
+    loads = [pltpu.make_async_copy(downs[i], wbuf[i], wsem.at[i]) for i in range(2)]
+    for load in loads:
+        load.start()
+    places, ring = four_places("split"), four_places("mp")
+    me, sib, far, diag = places
+    greet([{"mp": p} for p in ring[1:]] + [{"split": p} for p in places[1:]])
     links = Links(send, recv)
-    block = scale.shape[0] // mp
-    mine = rows_at(z, block)
+    block = count = scale.shape[0] // 4
+    mine = rows_at(ring[0], block)
     moves = []
     for diff, snd, rcv in zip(diffs, snds, rcvs):
         snd[...] = diff[...].astype(jnp.bfloat16)
         moves.append(
             [
-                links.copy(snd.at[rows_at(place, block)], rcv.at[k], {"mp": place})
-                for k, place in enumerate(places)
+                links.copy(snd.at[rows_at(p, block)], rcv.at[k], {"mp": p})
+                for k, p in enumerate(ring[1:])
             ]
         )
     factor = scale[mine, 0:1]
-    spread, sums = [], []
+    units = [Unit(links, sib, far, scratch[5 * i : 5 * i + 5]) for i in range(2)]
+    turns, sums = [], []
     for diff, rcv, cot, made in zip(diffs, rcvs, cots, moves):
         total = diff[mine, :]
         for k, move in enumerate(made):
@@ -304,70 +311,24 @@
             total = total + rcv[k].astype(jnp.float32)
         scaled = factor * total
         cot[mine, :] = scaled.astype(jnp.bfloat16)
+        turns.append(Spread(links, cot, block, ring, "mp"))
         sums.append(0.5 * jnp.sum(scaled * total, keepdims=True))
-        own = cot.at[mine]
-        spread += [links.copy(own, own, {"mp": place}) for place in places]
     row = lax.broadcasted_iota(jnp.int32, part.shape[1:], 0)
     part[0] = jnp.where(row == 0, sums[0], sums[1])
-    spread += [links.copy(part.at[0], part.at[k + 1], {"mp": p}) for k, p in enumerate(places)]
-    for move in spread:
-        move.wait_recv()
-    whole = part[0]
-    for k in range(1, mp):
-        whole = whole + part[k]
-    loss[...] = whole
-    links.drain()
-
-
-def cotangent_call(mp, diffs, scale):
-    rows, width = diffs[0].shape
-    block = rows // mp
-    shape = jax.ShapeDtypeStruct
-    return pl.pallas_call(
-        functools.partial(cotangent_kernel, mp),
-        out_shape=[shape((rows, width), jnp.bfloat16)] * 2 + [shape((8, 128), jnp.float32)],
-        in_specs=[VMEM] * 3,
-        out_specs=[VMEM] * 3,
-        scratch_shapes=[pltpu.VMEM((rows, width), jnp.bfloat16)] * 2
-        + [pltpu.VMEM((mp - 1, block, width), jnp.bfloat16)] * 2
-        + [pltpu.VMEM((mp, 8, 128), jnp.float32)]
-        + [pltpu.SemaphoreType.DMA((5 * (mp - 1),))] * 2,
-        compiler_params=pltpu.CompilerParams(
-            collective_id=1, has_side_effects=True, vmem_limit_bytes=GRANT
-        ),
-    )(*diffs, scale)
-
-
-def backward_kernel(*refs):
-    cots, downs, kept, part_in = refs[0:2], refs[2:4], refs[4:8], refs[8]
-    grads, loss = refs[9:13], refs[13]
-    xps, wbuf, part = refs[14:16], refs[16:18], refs[18]
-    send, recv, wsem = refs[-3:]
-    scratch = refs[19:-3]
-    loads = [pltpu.make_async_copy(downs[i], wbuf[i], wsem.at[i]) for i in range(2)]
-    for load in loads:
-        load.start()
-    me, sib, far, diag = split_places()
-    greet([{"split": place} for place in (sib, far, diag)])
-    links = Links(send, recv)
-    count = cots[0].shape[0] // 4
-    units = [Unit(links, sib, far, scratch[5 * i : 5 * i + 5]) for i in range(2)]
-    for i in range(2):
+    parts = [links.copy(part.at[0], part.at[k], {"mp": ring[k]}) for k in (1, 2, 3)]
+
+    def multiply(i):
+        turns[i].finish()
         arrange(xps[i], cots[i], (diag, sib, far, me), count)
         loads[i].wait()
         units[i].multiply(xps[i], wbuf[i], True)
-    part[0] = part_in[...]
-    marks = [
-        links.copy(part.at[0], part.at[k + 1], {"split": place})
-        for k, place in enumerate((sib, far, diag))
-    ]
-    units[0].forward()
-    units[1].forward()
+
     spreads = []
-    for i in range(2):
+
+    def differentiate(i):
         units[i].ready()
 
-        def body(cols, i=i):
+        def body(cols):
             back = units[i].value(cols)
             gate, up = kept[2 * i][:, cols], kept[2 * i + 1][:, cols]
             sig = jax.nn.sigmoid(gate)
@@ -376,10 +337,23 @@
             grads[2 * i + 1][rows_at(me, count), cols] = (back * gate * sig).astype(jnp.bfloat16)
 
         tiles(units[i].width, body)
-        spreads += [Spread(links, grads[2 * i + j], count, me, sib, far) for j in range(2)]
+        spreads.extend(Spread(links, grads[2 * i + j], count, places) for j in range(2))
+
+    turns[0].relay()
+    turns[1].relay()
+    multiply(0)
+    for move in parts:
+        move.wait_recv()
+    marked[0] = part[0] + part[1] + part[2] + part[3]
+    marks = [links.copy(marked.at[0], marked.at[k], {"split": places[k]}) for k in (1, 2, 3)]
+    units[0].forward()
+    multiply(1)
+    units[1].forward()
+    differentiate(0)
+    differentiate(1)
     for mark in marks:
         mark.wait_recv()
-    loss[...] = part[0] + part[1] + part[2] + part[3]
+    loss[...] = marked[0] + marked[1] + marked[2] + marked[3]
     for spread in spreads:
         spread.relay()
     for spread in spreads:
@@ -387,29 +361,33 @@
     links.drain()
 
 
-def backward_call(cots, downs, kept, part):
-    rows, width = cots[0].shape
+def backward_call(diffs, scale, downs, kept):
+    rows, width = diffs[0].shape
+    block = rows // 4
     widths = [down.shape[0] for down in downs]
     shape = jax.ShapeDtypeStruct
-    outs = [shape((rows, widths[i // 2]), jnp.bfloat16) for i in range(4)]
+    outs = [shape((rows, width), jnp.bfloat16)] * 2
+    outs += [shape((rows, widths[i // 2]), jnp.bfloat16) for i in range(4)]
     outs.append(shape((8, 128), jnp.float32))
     scratch = [pltpu.VMEM((rows, width), jnp.bfloat16)] * 2
+    scratch += [pltpu.VMEM((3, block, width), jnp.bfloat16)] * 2
+    scratch += [pltpu.VMEM((rows, width), jnp.bfloat16)] * 2
     scratch += [pltpu.VMEM(down.shape, jnp.bfloat16) for down in downs]
-    scratch += [pltpu.VMEM((4, 8, 128), jnp.float32)]
+    scratch += [pltpu.VMEM((4, 8, 128), jnp.float32)] * 2
     for w in widths:
         scratch += unit_scratch(rows, w)
-    copies = 2 * 2 + 3 * 4 + 3
+    copies = 2 * 3 + 2 * 3 + 3 + 2 * 2 + 3 * 4 + 3
     scratch += [pltpu.SemaphoreType.DMA((copies,))] * 2 + [pltpu.SemaphoreType.DMA((2,))]
     return pl.pallas_call(
         backward_kernel,
         out_shape=outs,
-        in_specs=[VMEM] * 2 + [ANY] * 2 + [VMEM] * 5,
-        out_specs=[VMEM] * 5,
+        in_specs=[VMEM] * 3 + [ANY] * 2 + [VMEM] * 4,
+        out_specs=[VMEM] * 7,
         scratch_shapes=scratch,
         compiler_params=pltpu.CompilerParams(
-            collective_id=2, has_side_effects=True, vmem_limit_bytes=GRANT
+            collective_id=1, has_side_effects=True, vmem_limit_bytes=GRANT
         ),
-    )(*cots, *downs, *kept, part)
+    )(*diffs, scale, *downs, *kept)
 
 
 def per_device_kernels(
@@ -441,8 +419,8 @@
     counted = jnp.sum(lengths).astype(jnp.float32)
     mask = valid_rows(lengths, gathered.shape[0])
     scale = jnp.broadcast_to(2.0 * mask / counted, (mask.shape[0], 128))
-    *cots, part = cotangent_call(mp, diffs, scale)
-    *grads_in, loss = backward_call(cots, (first_down, second_down), kept, part)
+    *made, loss = backward_call(diffs, scale, (first_down, second_down), kept)
+    cots, grads_in = made[:2], made[2:]
     downs = [contract_rows(hidden[i], cots[i]).astype(jnp.bfloat16) for i in range(2)]
     outs = []
     for item, flip in zip(grads_in, flips):
@@ -530,7 +508,7 @@
 
 def run(mp, split, *args):
     rows = args[0].shape[0] * mp
-    if split == 4 and mp > 1 and args[0].shape[0] % 16 == 0 and rows % 64 == 0:
+    if split == 4 and mp == 4 and args[0].shape[0] % 16 == 0 and rows % 64 == 0:
         return per_device_kernels(mp, *args)
     return per_device(*args)
 

time: 187 us -> 174 us (0.930)
  Pallas kernels: 151 us -> 139 us
    pallas_call x3 -> x2, Pallas kernels: 151 us -> 139 us  [the longest x1 72 us: backward_call(): pl.pallas_call(backward_kernel, out_shape=outs, in_specs=[VMEM] * 3 + [AN...]
where the time goes in v2:
time: 174 us
  Pallas kernels  139 us (80%)
  matrix products  30.6 us (18%)
  local copies, waits for them, and re-layouts  2.37 us (1%)
    pallas_call x1, Pallas kernels, backward_call(): pl.pallas_call(backward_kernel, out_shape=outs, in_specs=[VMEM] * 3 + [AN...  72 us
    pallas_call x1, Pallas kernels, forward_call(): pl.pallas_call(functools.partial(forward_kernel, flips), out_shape=outs,...  66.8 us
    dot_general x6, matrix products, contract_rows(): lax.dot_general(left, right, (((0,), (0,)), ((), ())), preferred_element_...  20.6 us
    dot_general x1, matrix products, per_device_kernels(): jnp.dot(hidden[2], teacher_down, preferred_element_type=jnp.float32)  6 us

profile of v2, /device:TPU:0, one launch (start us, length us, event | category | flops | bytes accessed | tf_op | source)
XLA Modules:
  0.0 173.9 jit_solution(6205232493686142911)
XLA Ops:
  0.6 66.8 %shard_map.162 = (bf16[192,1280]{1,0:T(8,128)(2,1)}, bf16[192,1728]{1,0:T(8,128)(2,1)}, bf16[192,1408]{1,0:T(8,128)(2,1)}, bf16[192,3456]{1,0:T(8,128)(2,1)}, f3...) custom-call(bf16[48,1280]{1,0:T(8,128)(2,1)} %refs_0_.1, ...), custom_call_target="tpu_custom_call" | custom-call | tf_op jit(solution)/shard_map/pallas_call | solution.py:267
  67.5 0.0 copy-start.1
  67.5 0.0 copy-start.3
  67.5 6.0 %fusion.1 = f32[192,1280]{1,0:T(8,128)S(1)} fusion(bf16[192,3456]{1,0:T(8,128)(2,1)} %get-tuple-element.24, bf16[3456,1280]{1,0:T(8,128)(2,1)} %param.15), kind=kOutput, calls=%fused_computation.18 | convolution fusion | flops 1698693120 | bytes 11157504 | tf_op jit(solution)/shard_map/dot_general | solution.py:414
  73.5 0.0 copy-start.2
  73.5 0.0 copy-start.4
  73.5 0.0 copy-done.1
  73.5 0.0 copy-done.3
  73.5 2.0 %convolution_subtract_fusion.1.refs_0_ = f32[192,1280]{1,0:T(8,128)} fusion(f32[192,1280]{1,0:T(8,128)S(1)} %fusion.1, bf16[192,1728]{1,0:T(8,128)(2,1)S(1)} %copy-done.3, bf16[1728,1280]{1,0:T(8,128)(2,1)S(1)} %copy-done.1), kind=kOutput, calls=%fused_computation.7 | convolution fusion | flops 849592320 | bytes 7053312 | tf_op jit(solution)/shard_map/dot_general | solution.py:416
  75.6 0.3 copy-done.4
  75.9 1.9 %convolution_subtract_fusion.refs_1_ = f32[192,1280]{1,0:T(8,128)} fusion(f32[192,1280]{1,0:T(8,128)S(1)} %fusion.1, bf16[192,1408]{1,0:T(8,128)(2,1)S(1)} %copy-done.4, bf16[1408,1280]{1,0:T(8,128)(2,1)S(1)} %copy-done.2), kind=kOutput, calls=%fused_computation.6 | convolution fusion | flops 692305920 | bytes 6111232 | tf_op jit(solution)/shard_map/dot_general | solution.py:417
  77.8 0.0 copy-done.10
  77.8 0.1 select_reduce_fusion
  77.9 0.6 reduce_sum.19
  79.2 0.7 broadcast_in_dim.23.refs_2_
  79.9 72.0 %shard_map.163 = (bf16[192,1280]{1,0:T(8,128)(2,1)}, bf16[192,1280]{1,0:T(8,128)(2,1)}, bf16[192,1728]{1,0:T(8,128)(2,1)}, bf16[192,1728]{1,0:T(8,128)(2,1)}, bf...) custom-call(f32[192,1280]{1,0:T(8,128)} %convolution_subtract_fusion.1.refs_0_, ...), custom_call_target="tpu_custom_call" | custom-call | tf_op jit(solution)/shard_map/pallas_call | solution.py:381
  152.0 4.6 %convolution_convert_fusion.5 = bf16[1280,1728]{0,1:T(8,128)(2,1)} fusion(bf16[192,1280]{1,0:T(8,128)(2,1)S(1)} %copy-done, bf16[192,1728]{1,0:T(8,128)(2,1)} %get-tuple-element.30), kind=kOutput, calls=%fused_computation.5 | convolution fusion | flops 851558400 | bytes 5578752 | tf_op jit(solution)/shard_map/dot_general | solution.py:20
  156.6 0.0 copy-done.5
  156.6 3.5 %convolution_convert_fusion.4 = bf16[1280,1728]{0,1:T(8,128)(2,1)} fusion(bf16[192,1280]{1,0:T(8,128)(2,1)S(1)} %copy-done, bf16[192,1728]{1,0:T(8,128)(2,1)S(1)} %copy-done.5), kind=kOutput, calls=%fused_computation.4 | convolution fusion | flops 851558400 | bytes 5578752 | tf_op jit(solution)/shard_map/dot_general | solution.py:20
  160.0 3.5 %convolution_convert_fusion.3 = bf16[1728,1280]{1,0:T(8,128)(2,1)} fusion(bf16[192,1728]{1,0:T(8,128)(2,1)S(1)} %copy-done.3, bf16[192,1280]{1,0:T(8,128)(2,1)S(1)} %copy-done.8), kind=kOutput, calls=%fused_computation.3 | convolution fusion | flops 851558400 | bytes 5578752 | tf_op jit(solution)/shard_map/dot_general | solution.py:20
  163.5 3.0 %convolution_convert_fusion.2 = bf16[1280,1408]{1,0:T(8,128)(2,1)} fusion(bf16[192,1280]{1,0:T(8,128)(2,1)S(1)} %copy-done, bf16[192,1408]{1,0:T(8,128)(2,1)S(1)} %copy-done.7), kind=kOutput, calls=%fused_computation.2 | convolution fusion | flops 693862400 | bytes 4636672 | tf_op jit(solution)/shard_map/dot_general | solution.py:20
  166.6 3.0 %convolution_convert_fusion.1 = bf16[1280,1408]{1,0:T(8,128)(2,1)} fusion(bf16[192,1280]{1,0:T(8,128)(2,1)S(1)} %copy-done, bf16[192,1408]{1,0:T(8,128)(2,1)S(1)} %copy-done.6), kind=kOutput, calls=%fused_computation.1 | convolution fusion | flops 693862400 | bytes 4636672 | tf_op jit(solution)/shard_map/dot_general | solution.py:20
  169.6 3.0 %convolution_convert_fusion = bf16[1408,1280]{1,0:T(8,128)(2,1)} fusion(bf16[192,1408]{1,0:T(8,128)(2,1)S(1)} %copy-done.4, bf16[192,1280]{1,0:T(8,128)(2,1)S(1)} %copy-done.9), kind=kOutput, calls=%fused_computation | convolution fusion | flops 693862400 | bytes 4636672 | tf_op jit(solution)/shard_map/dot_general | solution.py:20
  172.6 1.3 slice_reduce_fusion
  (15 shorter events, 0.0 us)
Async XLA Ops:
  67.5 6.1 %copy-start.1 = (bf16[1728,1280]{1,0:T(8,128)(2,1)S(1)}, bf16[1728,1280]{1,0:T(8,128)(2,1)}, u32[]{:S(2)}) copy-start(bf16[1728,1280]{1,0:T(8,128)(2,1)} %refs_3_.3) | copy-start | bytes 13271044
  67.5 6.1 %copy-start.3 = (bf16[192,1728]{1,0:T(8,128)(2,1)S(1)}, bf16[192,1728]{1,0:T(8,128)(2,1)}, u32[]{:S(2)}) copy-start(bf16[192,1728]{1,0:T(8,128)(2,1)} %get-tuple-element.23) | copy-start | bytes 1990660
  73.5 2.1 %copy-start.2 = (bf16[1408,1280]{1,0:T(8,128)(2,1)S(1)}, bf16[1408,1280]{1,0:T(8,128)(2,1)}, u32[]{:S(2)}) copy-start(bf16[1408,1280]{1,0:T(8,128)(2,1)} %refs_4_.3) | copy-start | bytes 10813444
  73.5 2.4 %copy-start.4 = (bf16[192,1408]{1,0:T(8,128)(2,1)S(1)}, bf16[192,1408]{1,0:T(8,128)(2,1)}, u32[]{:S(2)}) copy-start(bf16[192,1408]{1,0:T(8,128)(2,1)} %get-tuple-element.25) | copy-start | bytes 1622020
  75.6 2.2 %copy-start.10 = (s32[3]{0:T(128)S(1)}, s32[3]{0:T(128)}, u32[]{:S(2)}) copy-start(s32[3]{0:T(128)} %param.12) | copy-start | bytes 40
  79.9 72.0 %copy-start = (bf16[192,1280]{1,0:T(8,128)(2,1)S(1)}, bf16[192,1280]{1,0:T(8,128)(2,1)}, u32[]{:S(2)}) copy-start(bf16[192,1280]{1,0:T(8,128)(2,1)} %get-tuple-element.22) | copy-start | bytes 1474564
  151.9 4.6 %copy-start.5 = (bf16[192,1728]{1,0:T(8,128)(2,1)S(1)}, bf16[192,1728]{1,0:T(8,128)(2,1)}, u32[]{:S(2)}) copy-start(bf16[192,1728]{1,0:T(8,128)(2,1)} %get-tuple-element.31) | copy-start | bytes 1990660
  156.6 3.5 %copy-start.8 = (bf16[192,1280]{1,0:T(8,128)(2,1)S(1)}, bf16[192,1280]{1,0:T(8,128)(2,1)}, u32[]{:S(2)}) copy-start(bf16[192,1280]{1,0:T(8,128)(2,1)} %get-tuple-element.32) | copy-start | bytes 1474564
  160.0 3.5 %copy-start.7 = (bf16[192,1408]{1,0:T(8,128)(2,1)S(1)}, bf16[192,1408]{1,0:T(8,128)(2,1)}, u32[]{:S(2)}) copy-start(bf16[192,1408]{1,0:T(8,128)(2,1)} %get-tuple-element.33) | copy-start | bytes 1622020
  163.5 3.0 %copy-start.6 = (bf16[192,1408]{1,0:T(8,128)(2,1)S(1)}, bf16[192,1408]{1,0:T(8,128)(2,1)}, u32[]{:S(2)}) copy-start(bf16[192,1408]{1,0:T(8,128)(2,1)} %get-tuple-element.34) | copy-start | bytes 1622020
  166.6 3.1 %copy-start.9 = (bf16[192,1280]{1,0:T(8,128)(2,1)S(1)}, bf16[192,1280]{1,0:T(8,128)(2,1)}, u32[]{:S(2)}) copy-start(bf16[192,1280]{1,0:T(8,128)(2,1)} %get-tuple-element.35) | copy-start | bytes 1474564
